TPU v7x, 128 devices: a whole 4x4x4 slice. The times are simulated.
128 devices in a mesh: head: 16 (over y_lo, z, core), blk: 8 (over x, y_hi).
Axes of the slice: x: 4, y: 4 (y_hi: 2, y_lo: 2; y = y_hi * 2 + y_lo), z: 4, core: 2. Of those that a mesh axis runs over, the one named last changes fastest.
Arguments:
- query_head_matrix: bfloat16 [16384, 8192], P(('blk', 'head')), may hold values from -8 to 8
- key_matrix: bfloat16 [16384, 1024], P(('blk', 'head')), may hold values from -8 to 8
- value_matrix: bfloat16 [16384, 1024], P(('blk', 'head')), may hold values from -6 to 6
- output_gradient: bfloat16 [16384, 8192], P(('blk', 'head')), may hold values from -6 to 6
- span_lengths: int32 [62], replicated, may hold values from 1 to 512, 15872 in all
Outputs:
- attended: bfloat16 [16384, 8192], P(('blk', 'head'))
- query_grad: bfloat16 [16384, 8192], P(('blk', 'head'))
- key_gradient: bfloat16 [16384, 1024], P(('blk', 'head'))
- value_gradient: bfloat16 [16384, 1024], P(('blk', 'head'))
Inputs may be any that keep to these rules, and one draw needn't show every extreme that they name: `span_lengths`: the 62 span lengths sum to 15872, and the longest span holds exactly 512 tokens.
All inputs are finite; a program needn't handle non-finite values.
Results may differ from a plain program's by a relative error of at most 0.02.
Values may be sent and summed in bfloat16 or wider, within the bound.
No kernel may reach another device: no remote copies, remote signals or barrier semaphores. Data moves between devices by JAX's collectives and lax.ppermute only.
A program may use at most 128 MiB of HBM per device.

v0:
```python
import math

import jax
import jax.numpy as jnp
from jax import lax
from jax.sharding import PartitionSpec as P

QUERY_HEADS = 64
KEY_VALUE_HEADS = 8
HEAD_WIDTH = 128
QLEN = 512
MOST = 512


masked_score = -1e30


def passed_along(block, axis, distance):
    devices = range(lax.axis_size(axis))
    route = [(i - distance, i) for i in devices if i - distance in devices]
    return lax.ppermute(block, axis, route)


def broadcast(block, axis, holder):
    block = jnp.where(lax.axis_index(axis) == holder, block, jnp.zeros_like(block))
    return lax.psum(block, axis)


def merged_2(part, axis, combine):
    gathered = jax.tree.map(lambda a: lax.all_gather(a, axis), part)

    def take(source):
        return jax.tree.map(lambda a: lax.dynamic_index_in_dim(a, source, 0, False), gathered)

    return lax.fori_loop(
        1, lax.axis_size(axis), lambda source, state: combine(state, take(source)), take(0)
    )


def segment_of(span_lengths, positions, context):
    starts = jnp.cumsum(span_lengths) - span_lengths
    found_index = jnp.sum((starts[None, :] <= positions[:, None]).astype(jnp.int32), axis=1) - 1
    return jnp.where(positions >= context, span_lengths.shape[0], found_index)


def combine_parts(left_part, right_part):
    left_max, left_sum, left_acc = left_part
    right_max, right_sum, right_acc = right_part
    joint_max = jnp.maximum(left_max, right_max)
    left_factor = jnp.exp(left_max - joint_max)
    right_factor = jnp.exp(right_max - joint_max)
    joint_sum = left_sum * left_factor + right_sum * right_factor
    joint_acc = left_acc * left_factor[..., None] + right_acc * right_factor[..., None]
    return (joint_max, joint_sum, joint_acc)


def shards(query_head_matrix, key_matrix, value_matrix, output_gradient, span_lengths):
    head_total_count = lax.axis_size("head")
    cycle_count = lax.axis_size("blk")
    cycle_index = lax.axis_index("blk")
    local_token_count = query_head_matrix.shape[0]
    shard_rows = local_token_count * head_total_count
    context = shard_rows * cycle_count - QLEN
    local_heads = QUERY_HEADS // head_total_count
    replica_count = head_total_count // KEY_VALUE_HEADS
    tile_rows = min(512, shard_rows)
    tile_total = shard_rows // tile_rows
    score_scale = 1.0 / math.sqrt(HEAD_WIDTH)
    query_matrix = query_head_matrix.reshape(local_token_count, QUERY_HEADS, HEAD_WIDTH)
    output_adjoint = output_gradient.reshape(local_token_count, QUERY_HEADS, HEAD_WIDTH)
    key_head_rows = key_matrix.reshape(local_token_count, KEY_VALUE_HEADS, HEAD_WIDTH)
    value_head_rows = value_matrix.reshape(local_token_count, KEY_VALUE_HEADS, HEAD_WIDTH)
    key_send = jnp.repeat(key_head_rows, replica_count, axis=1)
    value_send = jnp.repeat(value_head_rows, replica_count, axis=1)
    query_head, grad_head, key_recv, value_recv = (
        lax.all_to_all(query_matrix, "head", split_axis=1, concat_axis=0, tiled=True),
        lax.all_to_all(output_adjoint, "head", split_axis=1, concat_axis=0, tiled=True),
        lax.all_to_all(key_send, "head", split_axis=1, concat_axis=0, tiled=True),
        lax.all_to_all(value_send, "head", split_axis=1, concat_axis=0, tiled=True),
    )
    key_local = key_recv.reshape(shard_rows, HEAD_WIDTH)
    value_local = value_recv.reshape(shard_rows, HEAD_WIDTH)
    rim_rows = jnp.stack([key_local[shard_rows - MOST :], value_local[shard_rows - MOST :]])
    rim_rows = passed_along(rim_rows, "blk", 1)
    key_window = jnp.concatenate([rim_rows[0], key_local])
    value_window = jnp.concatenate([rim_rows[1], value_local])
    base_row = cycle_index * shard_rows
    query_pos = base_row + jnp.arange(shard_rows, dtype=jnp.int32)
    window_pos = base_row - MOST + jnp.arange(shard_rows + MOST, dtype=jnp.int32)
    query_seg = segment_of(span_lengths, query_pos, context)
    window_seg = segment_of(span_lengths, window_pos, context)
    key_context = query_pos < context

    def tile_scores(tile_index):
        first_row = tile_index * tile_rows
        window_rows = tile_rows + MOST
        query_tile = lax.dynamic_slice_in_dim(query_head, first_row, tile_rows, 0)
        key_tile = lax.dynamic_slice_in_dim(key_window, first_row, window_rows, 0)
        value_tile = lax.dynamic_slice_in_dim(value_window, first_row, window_rows, 0)
        row_seg = lax.dynamic_slice_in_dim(query_seg, first_row, tile_rows, 0)
        row_pos = lax.dynamic_slice_in_dim(query_pos, first_row, tile_rows, 0)
        key_seg = lax.dynamic_slice_in_dim(window_seg, first_row, window_rows, 0)
        key_pos = lax.dynamic_slice_in_dim(window_pos, first_row, window_rows, 0)
        visible = (row_seg[:, None] == key_seg[None, :]) & (key_pos[None, :] <= row_pos[:, None])
        scores = (
            jnp.einsum("qhd,kd->hqk", query_tile, key_tile, preferred_element_type=jnp.float32)
            * score_scale
        )
        scores = jnp.where(visible[None], scores, masked_score)
        return (first_row, query_tile, key_tile, value_tile, visible, scores)

    def forward_tile(tile_index):
        first_row, query_tile, key_tile, value_tile, visible, scores = tile_scores(tile_index)
        row_max = jnp.max(scores, axis=2)
        weights = jnp.where(visible[None], jnp.exp(scores - row_max[..., None]), 0.0)
        row_total = jnp.sum(weights, axis=2)
        summed = jnp.einsum(
            "hqk,kd->qhd",
            weights.astype(jnp.bfloat16),
            value_tile,
            preferred_element_type=jnp.float32,
        )
        return (row_max.T, row_total.T, summed)

    tile_max, tile_sum, tile_acc = lax.map(forward_tile, jnp.arange(tile_total))
    tile_max = tile_max.reshape(shard_rows, local_heads)
    tile_sum = tile_sum.reshape(shard_rows, local_heads)
    tile_acc = tile_acc.reshape(shard_rows, local_heads, HEAD_WIDTH)
    question_start = shard_rows - QLEN
    last_cycle = cycle_count - 1
    own_rows = jnp.stack([query_head[question_start:], grad_head[question_start:]])
    shared_rows = broadcast(own_rows, "blk", last_cycle)
    question_query = jnp.moveaxis(shared_rows[0], 1, 0)
    question_grad = jnp.moveaxis(shared_rows[1], 1, 0)

    def question_forward(query_one):
        scores = (
            jnp.einsum("qd,kd->qk", query_one, key_local, preferred_element_type=jnp.float32)
            * score_scale
        )
        scores = jnp.where(key_context[None, :], scores, masked_score)
        row_max = jnp.max(scores, axis=1)
        weights = jnp.where(key_context[None, :], jnp.exp(scores - row_max[:, None]), 0.0)
        row_total = jnp.sum(weights, axis=1)
        summed = jnp.dot(
            weights.astype(jnp.bfloat16), value_local, preferred_element_type=jnp.float32
        )
        return (row_max, row_total, summed)

    part_max, part_sum, part_acc = lax.map(question_forward, question_query)
    merged = merged_2((part_max, part_sum, part_acc), "blk", combine_parts)
    holder = cycle_index == last_cycle
    own_stats = (
        tile_max[question_start:].T,
        tile_sum[question_start:].T,
        jnp.moveaxis(tile_acc[question_start:], 1, 0),
    )
    joined = combine_parts(own_stats, merged)
    question_max = jnp.where(holder, joined[0], own_stats[0]).T
    question_sum = jnp.where(holder, joined[1], own_stats[1]).T
    question_acc = jnp.moveaxis(jnp.where(holder, joined[2], own_stats[2]), 0, 1)
    row_max = jnp.concatenate([tile_max[:question_start], question_max])
    row_total = jnp.concatenate([tile_sum[:question_start], question_sum])
    row_acc = jnp.concatenate([tile_acc[:question_start], question_acc])
    attended_head = (row_acc / row_total[..., None]).astype(jnp.bfloat16)
    row_lse = row_max + jnp.log(row_total)
    attended_back = lax.all_to_all(attended_head, "head", split_axis=0, concat_axis=1, tiled=True)
    row_dd = jnp.sum(grad_head.astype(jnp.float32) * attended_head.astype(jnp.float32), axis=2)
    own_stat = jnp.stack([row_lse[question_start:].T, row_dd[question_start:].T])
    shared_stat = broadcast(own_stat, "blk", last_cycle)

    def backward_tile(running, tile_index):
        key_grads, value_grads = running
        first_row, query_tile, key_tile, value_tile, visible, scores = tile_scores(tile_index)
        lse_tile = lax.dynamic_slice_in_dim(row_lse, first_row, tile_rows, 0).T
        dd_tile = lax.dynamic_slice_in_dim(row_dd, first_row, tile_rows, 0).T
        grad_tile = lax.dynamic_slice_in_dim(grad_head, first_row, tile_rows, 0)
        probabilities = jnp.where(visible[None], jnp.exp(scores - lse_tile[..., None]), 0.0)
        value_part = jnp.einsum(
            "hqk,qhd->kd",
            probabilities.astype(jnp.bfloat16),
            grad_tile,
            preferred_element_type=jnp.float32,
        )
        prob_grad = jnp.einsum(
            "qhd,kd->hqk", grad_tile, value_tile, preferred_element_type=jnp.float32
        )
        score_grad = (probabilities * (prob_grad - dd_tile[..., None])).astype(jnp.bfloat16)
        query_part = (
            jnp.einsum("hqk,kd->qhd", score_grad, key_tile, preferred_element_type=jnp.float32)
            * score_scale
        )
        key_part = (
            jnp.einsum("hqk,qhd->kd", score_grad, query_tile, preferred_element_type=jnp.float32)
            * score_scale
        )
        window_rows = tile_rows + MOST
        key_grads = lax.dynamic_update_slice_in_dim(
            key_grads,
            lax.dynamic_slice_in_dim(key_grads, first_row, window_rows, 0) + key_part,
            first_row,
            0,
        )
        value_grads = lax.dynamic_update_slice_in_dim(
            value_grads,
            lax.dynamic_slice_in_dim(value_grads, first_row, window_rows, 0) + value_part,
            first_row,
            0,
        )
        return ((key_grads, value_grads), query_part)

    empty_window = jnp.zeros((shard_rows + MOST, HEAD_WIDTH), jnp.float32)
    (key_grads, value_grads), query_tiles = lax.scan(
        backward_tile, (empty_window, empty_window), jnp.arange(tile_total)
    )
    query_grads = query_tiles.reshape(shard_rows, local_heads, HEAD_WIDTH)

    def question_backward(parts):
        query_one, grad_one, lse_one, dd_one = parts
        scores = (
            jnp.einsum("qd,kd->qk", query_one, key_local, preferred_element_type=jnp.float32)
            * score_scale
        )
        probabilities = jnp.where(key_context[None, :], jnp.exp(scores - lse_one[:, None]), 0.0)
        value_part = jnp.einsum(
            "qk,qd->kd",
            probabilities.astype(jnp.bfloat16),
            grad_one,
            preferred_element_type=jnp.float32,
        )
        prob_grad = jnp.einsum(
            "qd,kd->qk", grad_one, value_local, preferred_element_type=jnp.float32
        )
        score_grad = (probabilities * (prob_grad - dd_one[:, None])).astype(jnp.bfloat16)
        query_part = (
            jnp.dot(score_grad, key_local, preferred_element_type=jnp.float32) * score_scale
        )
        key_part = (
            jnp.einsum("qk,qd->kd", score_grad, query_one, preferred_element_type=jnp.float32)
            * score_scale
        )
        return (query_part, key_part, value_part)

    quest_query_parts, quest_key_parts, quest_value_parts = lax.map(
        question_backward, (question_query, question_grad, shared_stat[0], shared_stat[1])
    )
    question_total = lax.psum(quest_query_parts, "blk")
    question_added = jnp.where(holder, jnp.moveaxis(question_total, 0, 1), 0.0)
    query_grads = jnp.concatenate(
        [query_grads[:question_start], query_grads[question_start:] + question_added]
    )
    dq_head = query_grads.astype(jnp.bfloat16)
    rim_grads = jnp.stack([key_grads[:MOST], value_grads[:MOST]])
    rim_back = passed_along(rim_grads, "blk", -1)
    tail_pad = jnp.zeros((shard_rows - MOST, HEAD_WIDTH), jnp.float32)
    key_total = (
        key_grads[MOST:]
        + jnp.sum(quest_key_parts, axis=0)
        + jnp.concatenate([tail_pad, rim_back[0]])
    )
    value_total = (
        value_grads[MOST:]
        + jnp.sum(quest_value_parts, axis=0)
        + jnp.concatenate([tail_pad, rim_back[1]])
    )
    grads_send = jnp.stack([key_total, value_total], axis=1)
    gradient_received = lax.all_to_all(grads_send, "head", split_axis=0, concat_axis=1, tiled=True)
    gradient_received = jnp.sum(
        gradient_received.reshape(local_token_count, KEY_VALUE_HEADS, replica_count, 2, HEAD_WIDTH),
        axis=2,
    )
    gradient_results = gradient_received.astype(jnp.bfloat16)
    key_gradient = gradient_results[:, :, 0].reshape(
        local_token_count, KEY_VALUE_HEADS * HEAD_WIDTH
    )
    value_gradient = gradient_results[:, :, 1].reshape(
        local_token_count, KEY_VALUE_HEADS * HEAD_WIDTH
    )
    query_back = lax.all_to_all(dq_head, "head", split_axis=0, concat_axis=1, tiled=True)
    attended = attended_back.reshape(local_token_count, QUERY_HEADS * HEAD_WIDTH)
    query_grad = query_back.reshape(local_token_count, QUERY_HEADS * HEAD_WIDTH)
    return (attended, query_grad, key_gradient, value_gradient)


def solution(mesh):
    in_specs = (
        P(("blk", "head"), None),
        P(("blk", "head"), None),
        P(("blk", "head"), None),
        P(("blk", "head"), None),
        P(),
    )
    out_specs = (
        P(("blk", "head"), None),
        P(("blk", "head"), None),
        P(("blk", "head"), None),
        P(("blk", "head"), None),
    )
    return jax.shard_map(shards, mesh=mesh, in_specs=in_specs, out_specs=out_specs, check_vma=False)
```

profile of v0, /device:TPU:1, one launch (start us, length us, event | category | flops | bytes accessed | tf_op | source)
XLA Modules:
  0.0 694.6 jit_solution(15561135243278335553)
XLA Ops:
  11.3 7.8 %all-to-all-start.2 = ((bf16[128,64,128]{0,2,1:T(8,128)(2,1)}), bf16[128,64,128]{0,2,1:T(8,128)(2,1)S(1)}, u32[]{:S(2)}, u32[]{:S(2)}) async-start(bf16[128,64,128]{0,2,1:T(8,128)(2,1)} %bitcast.404), calls=%async_computation.2 | async-start | bytes 4194304 | tf_op jit(solution)/shard_map/all_to_all | solution.py:76
  23.2 23.5 %all-to-all-done.2 = bf16[128,64,128]{0,2,1:T(8,128)(2,1)S(1)} async-done(((bf16[128,64,128]{0,2,1:T(8,128)(2,1)}), bf16[128,64,128]{0,2,1:T(8,128)(2,1)S(1)}, u32[]{:S(2)}, u32[]{:S(2)}) %all-to-all-start.2) | async-done | bytes 2097184 | tf_op jit(solution)/shard_map/all_to_all | solution.py:76
  48.0 6.3 all-to-all-start.3
  59.5 22.4 %all-to-all-done.3 = bf16[128,64,128]{0,2,1:T(8,128)(2,1)S(1)} async-done(((bf16[128,64,128]{0,2,1:T(8,128)(2,1)}), bf16[128,64,128]{0,2,1:T(8,128)(2,1)S(1)}, u32[]{:S(2)}, u32[]{:S(2)}) %all-to-all-start.3) | async-done | bytes 2097184 | tf_op jit(solution)/shard_map/all_to_all | solution.py:77
  88.0 6.3 all-to-all-start
  94.3 12.8 %all-to-all-done = bf16[128,16,128]{2,0,1:T(8,128)(2,1)S(1)} async-done(((bf16[128,16,128]{2,0,1:T(8,128)(2,1)}), bf16[128,16,128]{2,0,1:T(8,128)(2,1)S(1)}, u32[]{:S(2)}, u32[]{:S(2)}) %all-to-all-start) | async-done | bytes 524320 | tf_op jit(solution)/shard_map/all_to_all | solution.py:78
  112.4 62.5 %all-reduce.5.cloned.1.call-done = bf16[2,512,4,128]{3,1,2,0:T(8,128)(2,1)} async-done(((bf16[2,512,4,128]{3,1,2,0:T(8,128)(2,1)}), bf16[2,512,4,128]{3,1,2,0:T(8,128)(2,1)}) %all-reduce.5.cloned.1.call-update) | async-done | bytes 1048592 | tf_op jit(solution)/shard_map/psum | solution.py:26
  177.0 17.3 %while.80 = (s32[]{:T(128)}, f32[4,512]{1,0:T(4,128)S(1)}, f32[4,512]{1,0:T(4,128)}, f32[4,512,128]{2,1,0:T(8,128)S(1)}, bf16[4,512,128]{2,1,0:T(8,128)(2,1)S(1)...) while((s32[]{:T(128)}, f32[4,512]{1,0:T(4,128)S(1)}, ...), condition=%wide.region_11.12_spmd.clone, body=%wide.region_8.11_spmd.clone.sunk | while | flops 550505472 | bytes 14049409 | solution.py:150
  209.1 41.4 %while.77 = (s32[]{:T(128)}, f32[4,512,4]{1,2,0:T(4,128)S(1)}, f32[4,512,4]{1,2,0:T(4,128)S(1)}, f32[4,512,4,128]{1,3,2,0:T(8,128)}, s32[4]{0:T(128)S(1)}, /*ind...) while((s32[]{:T(128)}, f32[4,512,4]{1,2,0:T(4,128)S(1)}, ...), condition=%wide.region_6.7_spmd, body=%wide.region_3.6_spmd.sunk | while | flops 1102573568 | bytes 29462812 | solution.py:125
  215.2 4.3 fusion.178
  225.6 4.3 fusion.178
  250.6 5.5 copy.134
  256.0 5.4 copy.135
  266.0 30.1 %all-gather.3 = f32[8,4,512]{2,1,0:T(4,128)S(1)} all-gather(f32[1,4,512]{2,1,0:T(4,128)S(1)} %bitcast.429), channel_id=2, replica_groups=mesh['head'=16,'blk'=8] {'blk'}, dimensions={0}, use_global_device_ids=true | all-gather | bytes 73728 | tf_op jit(solution)/shard_map/all_gather | solution.py:30
  296.2 28.2 %all-gather.4 = f32[8,4,512]{2,1,0:T(4,128)S(1)} all-gather(f32[1,4,512]{2,1,0:T(4,128)S(1)} %bitcast.428), channel_id=3, replica_groups=mesh['head'=16,'blk'=8] {'blk'}, dimensions={0}, use_global_device_ids=true | all-gather | bytes 73728 | tf_op jit(solution)/shard_map/all_gather | solution.py:30
  325.7 15.1 %while.78 = (s32[]{:T(128)}, f32[4,512]{1,0:T(4,128)S(1)}, f32[4,512]{1,0:T(4,128)S(1)}, f32[4,512,128]{2,1,0:T(8,128)S(1)}, f32[8,4,512]{2,1,0:T(4,128)S(1)}, /...) while((s32[]{:T(128)}, f32[4,512]{1,0:T(4,128)S(1)}, ...), condition=%wide.region_13.14_spmd, body=%wide.region_12.13_spmd.sunk | while | flops 798725 | bytes 3227791 | solution.py:35
  348.2 32.9 %psum.22 = f32[2,4,512]{2,1,0:T(4,128)S(1)} all-reduce(f32[2,4,512]{2,1,0:T(4,128)S(1)} %maximum_select_fusion.1), channel_id=1, replica_groups=mesh['head'=16,'blk'=8] {'blk'}, use_global_device_ids=true, to_apply=%region_17.18 | all-reduce | flops 4096 | bytes 32768 | tf_op jit(solution)/shard_map/psum | solution.py:26
  381.6 4.6 copy.140
  386.3 30.8 %all-to-all-start.4 = ((bf16[2048,4,128]{2,1,0:T(4,128)(2,1)}), bf16[2048,4,128]{2,1,0:T(4,128)(2,1)}, u32[]{:S(2)}, u32[]{:S(2)}) async-start(bf16[2048,4,128]{2,1,0:T(4,128)(2,1)} %copy.140), calls=%async_computation.4 | async-start | bytes 4194304 | tf_op jit(solution)/shard_map/all_to_all | solution.py:167
  421.9 59.2 %while.79 = (s32[]{:T(128)}, f32[2560,128]{1,0:T(8,128)}, f32[2560,128]{1,0:T(8,128)}, f32[4,512,4,128]{1,3,2,0:T(8,128)}, s32[4]{0:T(128)S(1)}, /*index=5*/s32[...) while((s32[]{:T(128)}, f32[2560,128]{1,0:T(8,128)}, ...), condition=%wide.region_16.17_spmd, body=%wide.region_15.16_spmd.sunk | while | flops 2711748608 | bytes 74805720 | solution.py:213
  429.0 4.6 fusion.192
  443.8 4.6 fusion.192
  458.6 4.6 fusion.192
  473.4 4.6 fusion.192
  485.4 34.3 %while.81 = (s32[]{:T(128)}, f32[4,512,128]{2,1,0:T(8,128)S(1)}, f32[4,2048,128]{2,1,0:T(8,128)}, f32[4,2048,128]{2,1,0:T(8,128)}, bf16[4,512,128]{2,1,0:T(8,128...) while((s32[]{:T(128)}, f32[4,512,128]{2,1,0:T(8,128)S(1)}, ...), condition=%wide.region_19.20_spmd.clone, body=%wide.region_18.19_spmd.clone.sunk | while | flops 1349849088 | bytes 27543752 | solution.py:244
  532.4 5.7 all-to-all-start.6
  538.8 4.5 copy.146
  543.3 5.3 copy.147
  551.4 76.1 %all-reduce.7.cloned.1.call-done = f32[4,512,128]{2,1,0:T(8,128)} async-done(((f32[4,512,128]{2,1,0:T(8,128)}), f32[4,512,128]{2,1,0:T(8,128)}) %all-reduce.7.cloned.1.call-update) | async-done | bytes 1048592 | tf_op jit(solution)/shard_map/psum | solution.py:247
  630.4 10.7 %copy.148 = bf16[2048,4,128]{2,1,0:T(4,128)(2,1)} copy(bf16[2048,4,128]{2,0,1:T(8,128)(2,1)S(1)} %pad_maximum_fusion.1) | data formatting | bytes 4194304 | tf_op jit(solution)/shard_map/concatenate | solution.py:249
  641.1 10.5 %all-to-all-start.5 = ((bf16[2048,4,128]{2,1,0:T(4,128)(2,1)}), bf16[2048,4,128]{2,1,0:T(4,128)(2,1)}, u32[]{:S(2)}, u32[]{:S(2)}) async-start(bf16[2048,4,128]{2,1,0:T(4,128)(2,1)} %copy.148), calls=%async_computation.5 | async-start | bytes 4194304 | tf_op jit(solution)/shard_map/all_to_all | solution.py:279
  667.0 12.4 %all-to-all-done.5 = bf16[2048,4,128]{2,1,0:T(4,128)(2,1)} async-done(((bf16[2048,4,128]{2,1,0:T(4,128)(2,1)}), bf16[2048,4,128]{2,1,0:T(4,128)(2,1)}, u32[]{:S(2)}, u32[]{:S(2)}) %all-to-all-start.5) | async-done | bytes 2097184 | tf_op jit(solution)/shard_map/all_to_all | solution.py:279
  (359 shorter events, 242.8 us)
Async XLA Ops:
  7.2 79.9 %copy-start = (bf16[128,1024]{1,0:T(8,128)(2,1)S(1)}, bf16[128,1024]{1,0:T(8,128)(2,1)}, u32[]{:S(2)}) copy-start(bf16[128,1024]{1,0:T(8,128)(2,1)} %param.16) | copy-start | bytes 786436
  11.3 35.4 %all-to-all-start.2 = ((bf16[128,64,128]{0,2,1:T(8,128)(2,1)}), bf16[128,64,128]{0,2,1:T(8,128)(2,1)S(1)}, u32[]{:S(2)}, u32[]{:S(2)}) async-start(bf16[128,64,128]{0,2,1:T(8,128)(2,1)} %bitcast.404), calls=%async_computation.2 | async-start | bytes 4194304 | tf_op jit(solution)/shard_map/all_to_all | solution.py:76
  48.0 33.9 %all-to-all-start.3 = ((bf16[128,64,128]{0,2,1:T(8,128)(2,1)}), bf16[128,64,128]{0,2,1:T(8,128)(2,1)S(1)}, u32[]{:S(2)}, u32[]{:S(2)}) async-start(bf16[128,64,128]{0,2,1:T(8,128)(2,1)} %bitcast.403), calls=%async_computation.3 | async-start | bytes 4194304 | tf_op jit(solution)/shard_map/all_to_all | solution.py:77
  54.3 120.5 %all-reduce.5.cloned.1.call-start = ((), (), s32[]{:S(2)}) async-start(), calls=%async_computation.7 | async-start | bytes 2097152 | tf_op jit(solution)/shard_map/psum | solution.py:26
  81.9 5.1 copy-start.11
  84.8 9.5 %copy-start.23 = (bf16[128,1024]{1,0:T(8,128)(2,1)S(1)}, bf16[128,1024]{1,0:T(8,128)(2,1)}, u32[]{:S(2)}) copy-start(bf16[128,1024]{1,0:T(8,128)(2,1)} %param.17) | copy-start | bytes 786436
  88.0 19.1 %all-to-all-start = ((bf16[128,16,128]{2,0,1:T(8,128)(2,1)}), bf16[128,16,128]{2,0,1:T(8,128)(2,1)S(1)}, u32[]{:S(2)}, u32[]{:S(2)}) async-start(bf16[128,16,128]{2,0,1:T(8,128)(2,1)} %bitcast.26), calls=%async_computation | async-start | bytes 1048576 | tf_op jit(solution)/shard_map/all_to_all | solution.py:78
  108.1 68.9 %all-to-all-start.1 = ((bf16[128,16,128]{2,0,1:T(8,128)(2,1)}), bf16[128,16,128]{2,0,1:T(8,128)(2,1)S(1)}, u32[]{:S(2)}, u32[]{:S(2)}) async-start(bf16[128,16,128]{2,0,1:T(8,128)(2,1)} %bitcast.30), calls=%async_computation.1 | async-start | bytes 1048576 | tf_op jit(solution)/shard_map/all_to_all | solution.py:79
  112.3 212.1 %all-gather.7.cloned.1.call-start = ((), (), s32[]{:S(2)}) async-start(), calls=%async_computation.9 | async-start | bytes 9437184 | tf_op jit(solution)/shard_map/all_gather | solution.py:30
  177.0 18.4 %copy-start.33 = (s32[62]{0:T(128)S(1)}, s32[62]{0:T(128)}, u32[]{:S(2)}) copy-start(s32[62]{0:T(128)} %param.19) | copy-start | bytes 748
  194.4 9.1 %copy-start.6 = (bf16[2048,128]{1,0:T(8,128)(2,1)}, bf16[2048,128]{1,0:T(8,128)(2,1)S(1)}, u32[]{:S(2)}) copy-start(bf16[2048,128]{1,0:T(8,128)(2,1)S(1)} %get-tuple-element.1282) | copy-start | bytes 1572868
  194.4 9.0 %copy-start.14 = (bf16[4,512,128]{2,1,0:T(8,128)(2,1)}, bf16[4,512,128]{2,1,0:T(8,128)(2,1)S(1)}, u32[]{:S(2)}) copy-start(bf16[4,512,128]{2,1,0:T(8,128)(2,1)S(1)} %get-tuple-element.1296) | copy-start | bytes 1572868
  194.4 12.2 %copy-start.2 = (bf16[2048,128]{1,0:T(8,128)(2,1)}, bf16[2048,128]{1,0:T(8,128)(2,1)S(1)}, u32[]{:S(2)}) copy-start(bf16[2048,128]{1,0:T(8,128)(2,1)S(1)} %get-tuple-element.1278) | copy-start | bytes 1572868
  196.6 5.9 collective-permute-start
  203.4 5.7 copy-start.24
  203.4 5.7 copy-start.26
  203.4 5.7 copy-start.27
  203.5 5.7 copy-start.28
  203.5 5.7 copy-start.29
  250.6 5.5 copy-start.4
  265.3 30.8 %copy-start.30 = (f32[4,512]{1,0:T(4,128)S(1)}, f32[4,512]{1,0:T(4,128)}, u32[]{:S(2)}) copy-start(f32[4,512]{1,0:T(4,128)} %get-tuple-element.431) | copy-start | bytes 24580
  386.3 146.1 %all-to-all-start.4 = ((bf16[2048,4,128]{2,1,0:T(4,128)(2,1)}), bf16[2048,4,128]{2,1,0:T(4,128)(2,1)}, u32[]{:S(2)}, u32[]{:S(2)}) async-start(bf16[2048,4,128]{2,1,0:T(4,128)(2,1)} %copy.140), calls=%async_computation.4 | async-start | bytes 4194304 | tf_op jit(solution)/shard_map/all_to_all | solution.py:167
  417.1 4.9 copy-start.5
  421.9 63.4 %copy-start.3 = (bf16[2048,128]{1,0:T(8,128)(2,1)S(1)}, bf16[2048,128]{1,0:T(8,128)(2,1)}, u32[]{:S(2)}) copy-start(bf16[2048,128]{1,0:T(8,128)(2,1)} %copy-done.2) | copy-start | bytes 1572868
  473.4 4.7 copy-start.17
  473.4 4.7 copy-start.8
  484.0 43.8 %collective-permute-start.1 = (f32[2,512,128]{2,1,0:T(8,128)}, f32[2,512,128]{2,1,0:T(8,128)S(1)}, u32[]{:S(2)}, u32[]{:S(2)}) collective-permute-start(f32[2,512,128]{2,1,0:T(8,128)} %pad_maximum_fusion.5), channel_id=1, source_target_pairs={{1,0},{2,1},{3,2},{4,3},{5,4},{6,5},{7,6},{9,8},{10,9},{11,10},{12... | collective-permute-start | bytes 1572872 | tf_op jit(solution)/shard_map/ppermute | solution.py:21
  524.1 5.1 copy-start.10
  532.4 108.8 %all-to-all-start.6 = ((f32[2048,2,128]{2,1,0:T(2,128)}), f32[2048,2,128]{2,1,0:T(2,128)S(1)}, u32[]{:S(2)}, u32[]{:S(2)}) async-start(f32[2048,2,128]{2,1,0:T(2,128)} %pad_maximum_fusion.2), calls=%async_computation.6 | async-start | bytes 4194304 | tf_op jit(solution)/shard_map/all_to_all | solution.py:267
  538.1 89.4 %all-reduce.7.cloned.1.call-start = ((), (), s32[]{:S(2)}) async-start(), calls=%async_computation.8 | async-start | bytes 2097152 | tf_op jit(solution)/shard_map/psum | solution.py:247
  641.1 38.2 %all-to-all-start.5 = ((bf16[2048,4,128]{2,1,0:T(4,128)(2,1)}), bf16[2048,4,128]{2,1,0:T(4,128)(2,1)}, u32[]{:S(2)}, u32[]{:S(2)}) async-start(bf16[2048,4,128]{2,1,0:T(4,128)(2,1)} %copy.148), calls=%async_computation.5 | async-start | bytes 4194304 | tf_op jit(solution)/shard_map/all_to_all | solution.py:279
  681.2 6.7 copy-start.1
  (36 other events, 85.7 us)
Sparse Core Ops, SparseCore 0:
  87.2 87.6 all-reduce.4
  195.5 111.5 all-gather.6
  541.4 86.0 all-reduce.6
where the time goes:
time: 703 us; the launch traced here: 695 us
  waiting for transfers between devices  213 us (30%)
  local copies, waits for them, and re-layouts  124 us (18%)
  matrix products  108 us (15%)
  blocking collectives  91.2 us (13%)
  starting transfers between devices  76 us (11%)
  other arithmetic  62.5 us (9%)
  between operations  14.5 us (2%)
    psum x1, waiting for transfers between devices, shards(): question_total = lax.psum(quest_query_parts, 'blk')  76.1 us
    psum x1, waiting for transfers between devices, broadcast(): return lax.psum(block, axis)  62.5 us
    all_gather x2, blocking collectives, merged_2(): gathered = jax.tree.map(lambda a: lax.all_gather(a, axis), part)  58.3 us
    psum x1, blocking collectives, broadcast(): return lax.psum(block, axis)  32.9 us
    all_to_all x1, starting transfers between devices, shards(): lax.all_to_all(attended_head, 'head', split_axis=0, concat_axis=1, tiled=...  30.8 us
    all_to_all x1, waiting for transfers between devices, shards(): lax.all_to_all(query_matrix, 'head', split_axis=1, concat_axis=0, tiled=T...  23.5 us
    all_to_all x1, waiting for transfers between devices, shards(): lax.all_to_all(output_adjoint, 'head', split_axis=1, concat_axis=0, tiled...  22.4 us
    unnamed x60, local copies, waits for them, and re-layouts  22.1 us
  transfers between devices with their start and end apart: 12, of which 7 were waited for; matrix products, arithmetic and copies ran while one was open for 32% of the time, Pallas kernels for 0%

commit v1 on v0

v1 whole, which is shorter than its diff:
```python
import functools
import math

import jax
import jax.numpy as jnp
from jax import lax
from jax.experimental import pallas as pl
from jax.experimental.pallas import tpu as pltpu
from jax.sharding import Mesh
from jax.sharding import PartitionSpec as P

QUERY_HEADS = 64
KEY_VALUE_HEADS = 8
HEAD_WIDTH = 128
GROUP = QUERY_HEADS // KEY_VALUE_HEADS
QLEN = 512
ROWS = 128
BACK = 4
SPANS = 62
AXES = ("x", "yh", "yl", "z", "c")
MESH_AXES = ("yl", "z", "c", "x", "yh")
PLANE = ("x", "yh", "yl")
DEVICES = 128
CONTEXT = DEVICES * ROWS - QLEN
RING = 8 * ROWS
SCALE = 1.0 / math.sqrt(HEAD_WIDTH)
SCALE2 = SCALE * math.log2(math.e)
HIDDEN = -1e30
FLOOR = -1e29
BF16 = jnp.bfloat16
F32 = jnp.float32


def dot_nt(a, b):
    return lax.dot_general(a, b, (((1,), (1,)), ((), ())), preferred_element_type=F32)


def dot_nn(a, b):
    return lax.dot_general(a, b, (((1,), (0,)), ((), ())), preferred_element_type=F32)


def stacked(pair):
    return jnp.concatenate([pair[:, :HEAD_WIDTH], pair[:, HEAD_WIDTH:]], axis=0)


def unstacked(transposed):
    rows = transposed.T
    return jnp.concatenate([rows[:ROWS], rows[ROWS:]], axis=1).astype(BF16)


def context_kernel(
    place_ref, span_ref, q_ref, g_ref, kv0, kv1, kv2, kv3, kv4,
    out_ref, dq_ref, d0, d1, d2, d3, d4,
    bias, k_win, v_win, k_t, v_t, dk_acc, dv_acc,
):
    window = (BACK + 1) * ROWS
    group, pair = pl.program_id(0), pl.program_id(1)
    place = place_ref[0]

    @pl.when((group == 0) & (pair == 0))
    def _():
        row = place * ROWS + lax.broadcasted_iota(jnp.int32, (1, ROWS), 1)

        def step(n, carry):
            begin, start = carry
            start = jnp.where(row >= begin, begin, start)
            return begin + span_ref[n], start

        _, start = lax.fori_loop(0, SPANS, step, (jnp.int32(0), jnp.zeros((1, ROWS), jnp.int32)))
        start = jnp.where(row >= CONTEXT, DEVICES * ROWS, start)
        key = (place - BACK) * ROWS + lax.broadcasted_iota(jnp.int32, (window, ROWS), 0)
        bias[...] = jnp.where((key >= start) & (key <= row), 0.0, HIDDEN)

    @pl.when(pair == 0)
    def _():
        for i, ref in enumerate((kv4, kv3, kv2, kv1, kv0)):
            k_win[i * ROWS : (i + 1) * ROWS] = ref[0, 0]
            v_win[i * ROWS : (i + 1) * ROWS] = ref[0, 1]
            k_t[:, i * ROWS : (i + 1) * ROWS] = ref[0, 0].T
            v_t[:, i * ROWS : (i + 1) * ROWS] = ref[0, 1].T
        dk_acc[...] = jnp.zeros_like(dk_acc)
        dv_acc[...] = jnp.zeros_like(dv_acc)

    q = stacked(q_ref[...])
    g = stacked(g_ref[...])
    hide = jnp.concatenate([bias[...], bias[...]], axis=1)
    s = dot_nt(k_win[...], q) * SCALE2 + hide
    top = jnp.maximum(jnp.max(s, axis=0, keepdims=True), FLOOR)
    w = jnp.exp2(s - top)
    total = jnp.sum(w, axis=0, keepdims=True)
    p = w * jnp.where(total > 0.0, 1.0 / total, 0.0)
    dp = dot_nt(v_win[...], g)
    dd = jnp.sum(p * dp, axis=0, keepdims=True)
    ds = (p * (dp - dd)).astype(BF16)
    pb = p.astype(BF16)
    out_ref[...] = unstacked(dot_nn(v_t[...], pb))
    dq_ref[...] = unstacked(dot_nn(k_t[...], ds) * SCALE)
    dv_acc[...] += dot_nn(pb, g)
    dk_acc[...] += dot_nn(ds, q)

    @pl.when(pair == GROUP // 2 - 1)
    def _():
        for i, ref in enumerate((d4, d3, d2, d1, d0)):
            ref[0, 0] = (dk_acc[i * ROWS : (i + 1) * ROWS] * SCALE).astype(BF16)
            ref[0, 1] = dv_acc[i * ROWS : (i + 1) * ROWS].astype(BF16)


def context_attention(place, span_lengths, q, g, blocks):
    window = (BACK + 1) * ROWS
    wide = pl.BlockSpec((ROWS, 2 * HEAD_WIDTH), lambda a, b, *_: (0, a * (GROUP // 2) + b))
    block = pl.BlockSpec((1, 2, ROWS, HEAD_WIDTH), lambda a, b, *_: (a, 0, 0, 0))
    whole = jax.ShapeDtypeStruct(q.shape, BF16)
    part = jax.ShapeDtypeStruct((KEY_VALUE_HEADS, 2, ROWS, HEAD_WIDTH), BF16)
    return pl.pallas_call(
        context_kernel,
        grid_spec=pltpu.PrefetchScalarGridSpec(
            num_scalar_prefetch=2,
            grid=(KEY_VALUE_HEADS, GROUP // 2),
            in_specs=[wide, wide] + [block] * 5,
            out_specs=[wide, wide] + [block] * 5,
            scratch_shapes=[
                pltpu.VMEM((window, ROWS), F32),
                pltpu.VMEM((window, HEAD_WIDTH), BF16),
                pltpu.VMEM((window, HEAD_WIDTH), BF16),
                pltpu.VMEM((HEAD_WIDTH, window), BF16),
                pltpu.VMEM((HEAD_WIDTH, window), BF16),
                pltpu.VMEM((window, HEAD_WIDTH), F32),
                pltpu.VMEM((window, HEAD_WIDTH), F32),
            ],
        ),
        out_shape=[whole, whole] + [part] * 5,
        name="context_rows",
    )(place, span_lengths, q, g, *blocks)


def question_scores(ring_ref, k, q, half):
    wide = q.shape[0]
    s = dot_nt(k, q) * SCALE2
    r = half * wide + lax.broadcasted_iota(jnp.int32, (1, wide), 1)
    row = CONTEXT + (r // 8) % 4 * ROWS + r // 32 * 8 + r % 8
    key = ring_ref[0] * RING + lax.broadcasted_iota(jnp.int32, s.shape, 0)
    return jnp.where(key <= row, s, HIDDEN)


def question_half(qg_ref, half, which):
    part = qg_ref[:, which]
    return part.reshape(part.shape[0] * part.shape[1], HEAD_WIDTH)


def statistics_kernel(ring_ref, qg_ref, kv_ref, stats_ref):
    head, half = pl.program_id(0), pl.program_id(1)
    k = kv_ref[:, 0].reshape(RING, HEAD_WIDTH)
    v = kv_ref[:, 1].reshape(RING, HEAD_WIDTH)
    q = question_half(qg_ref, half, 0)
    g = question_half(qg_ref, half, 1)
    s = question_scores(ring_ref, k, q, half)
    top = jnp.max(s, axis=0, keepdims=True)
    w = jnp.exp2(s - top)
    total = jnp.sum(w, axis=0, keepdims=True)
    dd = jnp.sum(w * dot_nt(v, g), axis=0, keepdims=True)
    stats_ref[pl.ds(head, 1), :] = top
    stats_ref[pl.ds(GROUP + head, 1), :] = total
    stats_ref[pl.ds(2 * GROUP + head, 1), :] = dd


def question_kernel(ring_ref, qg_ref, kv_ref, stats_ref, part_ref, dkv_ref, k_t, v_t, dk_acc, dv_acc):
    head, half = pl.program_id(0), pl.program_id(1)
    k = kv_ref[:, 0].reshape(RING, HEAD_WIDTH)
    v = kv_ref[:, 1].reshape(RING, HEAD_WIDTH)

    @pl.when((head == 0) & (half == 0))
    def _():
        k_t[...] = k.T
        v_t[...] = v.T
        dk_acc[...] = jnp.zeros_like(dk_acc)
        dv_acc[...] = jnp.zeros_like(dv_acc)

    q = question_half(qg_ref, half, 0)
    g = question_half(qg_ref, half, 1)
    s = question_scores(ring_ref, k, q, half)
    lse = stats_ref[pl.ds(head, 1), :]
    dd = stats_ref[pl.ds(GROUP + head, 1), :]
    p = jnp.exp2(s - lse)
    ds = (p * (dot_nt(v, g) - dd)).astype(BF16)
    pb = p.astype(BF16)
    shape = (part_ref.shape[0], part_ref.shape[2], HEAD_WIDTH)
    part_ref[:, 0] = dot_nn(v_t[...], pb).T.astype(BF16).reshape(shape)
    part_ref[:, 1] = (dot_nn(k_t[...], ds) * SCALE).T.astype(BF16).reshape(shape)
    dv_acc[...] += dot_nn(pb, g)
    dk_acc[...] += dot_nn(ds, q)

    @pl.when((head == GROUP - 1) & (half == 1))
    def _():
        dkv_ref[:, 0] = (dk_acc[...] * SCALE).astype(BF16).reshape(8, ROWS, HEAD_WIDTH)
        dkv_ref[:, 1] = dv_acc[...].astype(BF16).reshape(8, ROWS, HEAD_WIDTH)


def question_specs():
    rows = pl.BlockSpec((8, 2, 32, HEAD_WIDTH), lambda h, c, *_: (c, 0, 0, h))
    keys = pl.BlockSpec((8, 2, ROWS, HEAD_WIDTH), lambda h, c, *_: (0, 0, 0, 0))
    return rows, keys


def question_statistics(ring, qg, kv):
    rows, keys = question_specs()
    return pl.pallas_call(
        statistics_kernel,
        grid_spec=pltpu.PrefetchScalarGridSpec(
            num_scalar_prefetch=1,
            grid=(GROUP, 2),
            in_specs=[rows, keys],
            out_specs=pl.BlockSpec((3 * GROUP, QLEN // 2), lambda h, c, *_: (0, c)),
        ),
        out_shape=jax.ShapeDtypeStruct((3 * GROUP, QLEN), F32),
        name="question_statistics",
    )(ring, qg, kv)


def question_attention(ring, qg, kv, stats):
    rows, keys = question_specs()
    return pl.pallas_call(
        question_kernel,
        grid_spec=pltpu.PrefetchScalarGridSpec(
            num_scalar_prefetch=1,
            grid=(GROUP, 2),
            in_specs=[rows, keys, pl.BlockSpec((2 * GROUP, QLEN // 2), lambda h, c, *_: (0, c))],
            out_specs=[rows, keys],
            scratch_shapes=[
                pltpu.VMEM((HEAD_WIDTH, RING), BF16),
                pltpu.VMEM((HEAD_WIDTH, RING), BF16),
                pltpu.VMEM((RING, HEAD_WIDTH), F32),
                pltpu.VMEM((RING, HEAD_WIDTH), F32),
            ],
        ),
        out_shape=[
            jax.ShapeDtypeStruct(qg.shape, BF16),
            jax.ShapeDtypeStruct(kv.shape, BF16),
        ],
        name="question_rows",
    )(ring, qg, kv, stats)


def shifted(block, distance):
    index = [place % 16 * 8 + place // 16 for place in range(DEVICES)]
    route = [(index[i], index[(i + distance) % DEVICES]) for i in range(DEVICES)]
    return lax.ppermute(block, MESH_AXES, route)


def exchanged(blocks, axes):
    return lax.all_to_all(blocks, axes, split_axis=0, concat_axis=0, tiled=True)


def merged(stats, axis):
    parts = lax.all_gather(stats, axis)
    tops, totals, sums = jnp.split(parts, 3, axis=1)
    top = jnp.max(tops, axis=0)
    factor = jnp.exp2(tops - top)
    return jnp.concatenate([top, jnp.sum(totals * factor, axis=0), jnp.sum(sums * factor, axis=0)])


def shards(q, k, v, g, span_lengths):
    place = lax.axis_index(AXES)
    ring = place // 8
    ring_arg = ring.reshape(1).astype(jnp.int32)
    place_arg = place.reshape(1).astype(jnp.int32)
    last = place >= DEVICES - 4

    def dealt(a):
        return a.reshape(16, 8, KEY_VALUE_HEADS, GROUP * HEAD_WIDTH).transpose(0, 2, 1, 3)

    deal = jnp.stack([dealt(q), dealt(g)], axis=2).reshape(DEVICES, 2, 8, GROUP * HEAD_WIDTH)
    own = exchanged(deal, AXES)[DEVICES - 4 :]
    own = own.transpose(1, 0, 2, 3).reshape(1, 2, 32, GROUP * HEAD_WIDTH)
    qg = exchanged(jnp.broadcast_to(own, (16,) + own.shape[1:]), PLANE)

    def headed(a):
        return a.reshape(ROWS, KEY_VALUE_HEADS, HEAD_WIDTH).transpose(1, 0, 2)

    kv = jnp.stack([headed(k), headed(v)], axis=1)
    kv_ring = exchanged(kv, ("z", "c"))
    kv1, kv2 = shifted(kv, 1), shifted(kv, 2)
    kv3, kv4 = shifted(kv1, 2), shifted(kv2, 2)

    out, dq, d0, d1, d2, d3, d4 = context_attention(
        place_arg, span_lengths, q, g, (kv, kv1, kv2, kv3, kv4)
    )
    stats = merged(merged(question_statistics(ring_arg, qg, kv_ring), ("yh", "yl")), "x")
    top, total, sums = jnp.split(stats, 3)
    stats = jnp.concatenate([top + jnp.log2(total), sums / total])
    parts, dkv_ring = question_attention(ring_arg, qg, kv_ring, stats)

    def added(*terms):
        return sum(t.astype(F32) for t in terms)

    r3, r4 = shifted(d3, -2), shifted(d4, -2)
    r1 = shifted(added(d1, r3).astype(BF16), -1)
    r2 = shifted(added(d2, r4).astype(BF16), -2)
    dkv = added(d0, r1, r2, exchanged(dkv_ring, ("z", "c"))).astype(BF16)
    dk = dkv[:, 0].transpose(1, 0, 2).reshape(k.shape)
    dv = dkv[:, 1].transpose(1, 0, 2).reshape(v.shape)

    summed = jnp.sum(exchanged(parts, PLANE).astype(F32), axis=0).astype(BF16)
    summed = summed.reshape(2, 4, 8, GROUP * HEAD_WIDTH).transpose(1, 0, 2, 3)
    rest = jnp.zeros((DEVICES - 4,) + summed.shape[1:], BF16)
    back = exchanged(jnp.concatenate([rest, summed]), AXES)
    back = back.reshape(16, KEY_VALUE_HEADS, 2, 8, GROUP * HEAD_WIDTH).transpose(2, 0, 3, 1, 4)
    back = back.reshape(2, ROWS, QUERY_HEADS * HEAD_WIDTH)
    return jnp.where(last, back[0], out), jnp.where(last, back[1], dq), dk, dv


def solution(mesh):
    grid = Mesh(mesh.devices.reshape(2, 4, 2, 4, 2), MESH_AXES)
    rows = P(AXES, None)
    return jax.shard_map(
        shards,
        mesh=grid,
        in_specs=(rows, rows, rows, rows, P()),
        out_specs=(rows,) * 4,
        check_vma=False,
    )
```

time: 703 us -> 410 us (0.58)
  local copies, waits for them, and re-layouts: 124 us -> 14.8 us
  matrix products: 108 us -> 0 us
  Pallas kernels: 0 us -> 74.5 us
  other arithmetic: 62.5 us -> 11.7 us
  blocking collectives: 91.2 us -> 41.7 us
  starting transfers between devices: 76 us -> 60.3 us
  between operations: 14.5 us -> 0.86 us
  waiting for transfers between devices: 213 us -> 205 us
    psum x2 -> x0, waiting for transfers between devices: 139 us -> none  [the longest x1 76.1 us: shards(): question_total = lax.psum(quest_query_parts, 'blk')]
    dot_general x56 -> x0, matrix products: 108 us -> none  [the longest x4 18.6 us: backward_tile(): jnp.einsum('qhd,kd->hqk', grad_tile, value_tile, preferred_element_type=j...]
    ppermute x2 -> x8, waiting for transfers between devices: 2.31 us -> 111 us  [shifted(): return lax.ppermute(block, MESH_AXES, route)]
    pallas_call x0 -> x3, Pallas kernels: none -> 74.5 us  [the longest x1 41.4 us: context_attention(): pl.pallas_call(context_kernel, grid_spec=pltpu.PrefetchScalarGridSpec(num...]
    all_gather x2, blocking collectives: 58.3 us -> 19 us  [merged(): parts = lax.all_gather(stats, axis)]
    psum x1 -> x0, blocking collectives: 32.9 us -> none  [broadcast(): return lax.psum(block, axis)]
    all_to_all x7 -> x5, starting transfers between devices: 71.6 us -> 39.4 us  [exchanged(): return lax.all_to_all(blocks, axes, split_axis=0, concat_axis=0, tiled=True)]
    all_to_all x8 -> x0, local copies, waits for them, and re-layouts: 25.5 us -> none  [the longest x2 7.14 us: shards(): lax.all_to_all(query_matrix, 'head', split_axis=1, concat_axis=0, tiled=T...]
  transfers between devices with their start and end apart: 12 -> 13, of which waited for: 7 -> 11; matrix products, arithmetic and copies ran while one was open for 32% -> 3% of each run, Pallas kernels for 0% -> 10%
where the time goes in v1:
time: 410 us; the launch traced here: 409 us
  waiting for transfers between devices  205 us (50%)
  Pallas kernels  74.5 us (18%)
  starting transfers between devices  60.3 us (15%)
  blocking collectives  41.7 us (10%)
  local copies, waits for them, and re-layouts  14.8 us (4%)
  other arithmetic  11.7 us (3%)
    ppermute x8, waiting for transfers between devices, shifted(): return lax.ppermute(block, MESH_AXES, route)  111 us
    all_to_all x5, waiting for transfers between devices, exchanged(): return lax.all_to_all(blocks, axes, split_axis=0, concat_axis=0, tiled=True)  94.1 us
    pallas_call x1, Pallas kernels, context_attention(): pl.pallas_call(context_kernel, grid_spec=pltpu.PrefetchScalarGridSpec(num...  41.4 us
    all_to_all x5, starting transfers between devices, exchanged(): return lax.all_to_all(blocks, axes, split_axis=0, concat_axis=0, tiled=True)  39.4 us
    all_to_all x1, blocking collectives, exchanged(): return lax.all_to_all(blocks, axes, split_axis=0, concat_axis=0, tiled=True)  22.7 us
    ppermute x8, starting transfers between devices, shifted(): return lax.ppermute(block, MESH_AXES, route)  20.9 us
    all_gather x2, blocking collectives, merged(): parts = lax.all_gather(stats, axis)  19 us
    pallas_call x1, Pallas kernels, question_attention(): pl.pallas_call(question_kernel, grid_spec=pltpu.PrefetchScalarGridSpec(nu...  18.7 us
  transfers between devices with their start and end apart: 13, of which 11 were waited for; matrix products, arithmetic and copies ran while one was open for 3% of the time, Pallas kernels for 10%

profile of v1, /device:TPU:1, one launch (start us, length us, event | category | flops | bytes accessed | tf_op | source)
XLA Modules:
  0.0 408.6 jit_solution(8999968619501303642)
XLA Ops:
  0.6 4.6 %pad_maximum_fusion = bf16[128,2,8,1024]{3,2,1,0:T(8,128)(2,1)} fusion(bf16[128,1,8,1024]{3,2,1,0:T(8,128)(2,1)} %bitcast.48, bf16[128,1,8,1024]{3,2,1,0:T(8,128)(2,1)} %bitcast.49), kind=kLoop, calls=%fused_computation | loop fusion | flops 2097152 | bytes 8388608 | tf_op jit(solution)/shard_map/stack | solution.py:271
  5.2 11.9 %all-to-all-start = ((bf16[128,2,8,1024]{3,2,1,0:T(8,128)(2,1)}), bf16[128,2,8,1024]{3,2,1,0:T(8,128)(2,1)}, u32[]{:S(2)}, u32[]{:S(2)}) async-start(bf16[128,2,8,1024]{3,2,1,0:T(8,128)(2,1)} %pad_maximum_fusion), calls=%async_computation | async-start | bytes 8388608 | tf_op jit(solution)/shard_map/all_to_all | solution.py:250
  18.8 51.1 %all-to-all-done = bf16[128,2,8,1024]{3,2,1,0:T(8,128)(2,1)} async-done(((bf16[128,2,8,1024]{3,2,1,0:T(8,128)(2,1)}), bf16[128,2,8,1024]{3,2,1,0:T(8,128)(2,1)}, u32[]{:S(2)}, u32[]{:S(2)}) %all-to-all-start) | async-done | bytes 4194336 | tf_op jit(solution)/shard_map/all_to_all | solution.py:250
  69.9 4.5 %all-to-all-start.2 = ((bf16[8,2,128,128]{3,2,1,0:T(8,128)(2,1)}), bf16[8,2,128,128]{3,2,1,0:T(8,128)(2,1)S(1)}, u32[]{:S(2)}, u32[]{:S(2)}) async-start(bf16[8,2,128,128]{3,2,1,0:T(8,128)(2,1)} %pad_maximum_fusion.1.kv0), calls=%async_computation.2 | async-start | bytes 1048576 | tf_op jit(solution)/shard_map/all_to_all | solution.py:250
  75.3 8.5 %all-to-all-done.2.kv_ref = bf16[8,2,128,128]{3,2,1,0:T(8,128)(2,1)S(1)} async-done(((bf16[8,2,128,128]{3,2,1,0:T(8,128)(2,1)}), bf16[8,2,128,128]{3,2,1,0:T(8,128)(2,1)S(1)}, u32[]{:S(2)}, u32[]{:S(2)}) %all-to-all-start.2) | async-done | bytes 524320 | tf_op jit(solution)/shard_map/all_to_all | solution.py:250
  83.8 1.6 broadcast_in_dim.5
  85.4 3.7 all-to-all-start.1
  89.1 28.1 %all-to-all-done.1.qg_ref = bf16[16,2,32,1024]{3,2,1,0:T(8,128)(2,1)S(1)} async-done(((bf16[16,2,32,1024]{3,2,1,0:T(8,128)(2,1)}), bf16[16,2,32,1024]{3,2,1,0:T(8,128)(2,1)S(1)}, u32[]{:S(2)}, u32[]{:S(2)}) %all-to-all-start.1) | async-done | bytes 2097184 | tf_op jit(solution)/shard_map/all_to_all | solution.py:250
  118.6 14.4 %question_statistics.1 = f32[24,512]{1,0:T(8,128)} custom-call(s32[1]{0:T(128)} %bitcast.ring_ref, bf16[16,2,32,1024]{3,2,1,0:T(8,128)(2,1)} %copy-done, bf16[8,2,128,128]{3,2,1,0:T(8,128)(2,1)} %copy-done.1), custom_call_target="tpu_custom_call" | custom-call | tf_op jit(solution)/shard_map/question_statistics/pallas_call | solution.py:206
  133.0 9.8 %all-gather = f32[96,512]{1,0:T(8,128)S(1)} all-gather(f32[24,512]{1,0:T(8,128)} %question_statistics.1), channel_id=2, replica_groups=mesh['yl'=2,'z'=4,'c'=2,'x'=4,'yh'=2] {'yh','yl'}, dimensions={0}, use_global_device_ids=true | all-gather | bytes 245760 | tf_op jit(solution)/shard_map/all_gather | solution.py:254
  142.8 9.2 %all-gather.1 = f32[96,512]{1,0:T(8,128)S(1)} all-gather(f32[24,512]{1,0:T(8,128)S(1)} %pad_maximum_fusion.2), channel_id=3, replica_groups=mesh['yl'=2,'z'=4,'c'=2,'x'=4,'yh'=2] {'x'}, dimensions={0}, use_global_device_ids=true | all-gather | bytes 245760 | tf_op jit(solution)/shard_map/all_gather | solution.py:254
  152.7 18.7 %question_rows.1 = (bf16[16,2,32,1024]{3,2,1,0:T(8,128)(2,1)}, bf16[8,2,128,128]{3,2,1,0:T(8,128)(2,1)}) custom-call(s32[1]{0:T(128)} %bitcast.ring_ref, bf16[16,2,32,1024]{3,2,1,0:T(8,128)(2,1)} %copy-done, bf16[8,2,128,128]{3,2,1,0:T(8,128)(2,1)} %copy-done.1, f32[16,512]{1,0:T(8,128)} %pad_maximum_fusion.3.stats_ref), custom_call_target="tpu_custom_call" | custom-call | tf_op jit(solution)/shard_map/question_rows/pallas_call | solution.py:221
  171.4 22.7 %all_to_all.30 = bf16[16,2,32,1024]{3,2,1,0:T(8,128)(2,1)S(1)} all-to-all(bf16[16,2,32,1024]{3,2,1,0:T(8,128)(2,1)} %get-tuple-element.13), channel_id=1, replica_groups=mesh['yl'=2,'z'=4,'c'=2,'x'=4,'yh'=2] {'x','yh','yl'}, dimensions={0} | all-to-all | bytes 4194304 | tf_op jit(solution)/shard_map/all_to_all | solution.py:250
  194.1 13.7 %all-to-all-start.5 = ((bf16[8,2,128,128]{3,2,1,0:T(8,128)(2,1)}), bf16[8,2,128,128]{3,2,1,0:T(8,128)(2,1)S(1)}, u32[]{:S(2)}, u32[]{:S(2)}) async-start(bf16[8,2,128,128]{3,2,1,0:T(8,128)(2,1)} %get-tuple-element.21), calls=%async_computation.5 | async-start | bytes 1048576 | tf_op jit(solution)/shard_map/all_to_all | solution.py:250
  208.3 2.5 concatenate.12.clone
  210.8 6.5 %all-to-all-done.5 = bf16[8,2,128,128]{3,2,1,0:T(8,128)(2,1)S(1)} async-done(((bf16[8,2,128,128]{3,2,1,0:T(8,128)(2,1)}), bf16[8,2,128,128]{3,2,1,0:T(8,128)(2,1)S(1)}, u32[]{:S(2)}, u32[]{:S(2)}) %all-to-all-start.5) | async-done | bytes 524320 | tf_op jit(solution)/shard_map/all_to_all | solution.py:250
  217.2 5.5 %all-to-all-start.4 = ((bf16[128,2,8,1024]{3,2,1,0:T(8,128)(2,1)}), bf16[128,2,8,1024]{3,2,1,0:T(8,128)(2,1)}, u32[]{:S(2)}, u32[]{:S(2)}) async-start(bf16[128,2,8,1024]{3,2,1,0:T(8,128)(2,1)} %concatenate.12.clone), calls=%async_computation.4 | async-start | bytes 8388608 | tf_op jit(solution)/shard_map/all_to_all | solution.py:250
  222.7 2.0 collective-permute-start
  226.2 52.3 %collective-permute-done.kv1 = bf16[8,2,128,128]{3,2,1,0:T(8,128)(2,1)S(1)} collective-permute-done((bf16[8,2,128,128]{3,2,1,0:T(8,128)(2,1)}, bf16[8,2,128,128]{3,2,1,0:T(8,128)(2,1)S(1)}, u32[]{:S(2)}, u32[]{:S(2)}) %collective-permute-start) | collective-permute-done | bytes 524320 | tf_op jit(solution)/shard_map/ppermute | solution.py:246
  278.5 2.1 collective-permute-start.2
  280.6 12.1 %collective-permute-done.1.kv2 = bf16[8,2,128,128]{3,2,1,0:T(8,128)(2,1)S(1)} collective-permute-done((bf16[8,2,128,128]{3,2,1,0:T(8,128)(2,1)}, bf16[8,2,128,128]{3,2,1,0:T(8,128)(2,1)S(1)}, u32[]{:S(2)}, u32[]{:S(2)}) %collective-permute-start.1) | collective-permute-done | bytes 524320 | tf_op jit(solution)/shard_map/ppermute | solution.py:246
  292.7 8.3 %collective-permute-done.2.kv3 = bf16[8,2,128,128]{3,2,1,0:T(8,128)(2,1)S(1)} collective-permute-done((bf16[8,2,128,128]{3,2,1,0:T(8,128)(2,1)S(1)}, bf16[8,2,128,128]{3,2,1,0:T(8,128)(2,1)S(1)}, u32[]{:S(2)}, u32[]{:S(2)}) %collective-permute-start.2) | collective-permute-done | bytes 524320 | tf_op jit(solution)/shard_map/ppermute | solution.py:246
  301.0 11.2 %collective-permute-done.3.kv4 = bf16[8,2,128,128]{3,2,1,0:T(8,128)(2,1)S(1)} collective-permute-done((bf16[8,2,128,128]{3,2,1,0:T(8,128)(2,1)S(1)}, bf16[8,2,128,128]{3,2,1,0:T(8,128)(2,1)S(1)}, u32[]{:S(2)}, u32[]{:S(2)}) %collective-permute-start.3) | collective-permute-done | bytes 524320 | tf_op jit(solution)/shard_map/ppermute | solution.py:246
  313.0 41.4 %context_rows.1 = (bf16[128,8192]{1,0:T(8,128)(2,1)}, bf16[128,8192]{1,0:T(8,128)(2,1)}, bf16[8,2,128,128]{3,2,1,0:T(8,128)(2,1)}, bf16[8,2,128,128]{3,2,1,0:T(8...) custom-call(s32[1]{0:T(128)} %bitcast.22.place_ref, ...), custom_call_target="tpu_custom_call" | custom-call | tf_op jit(solution)/shard_map/context_rows/pallas_call | solution.py:114
  354.4 3.1 collective-permute-start.4
  357.7 11.0 %collective-permute-done.4 = bf16[8,2,128,128]{3,2,1,0:T(8,128)(2,1)S(1)} collective-permute-done((bf16[8,2,128,128]{3,2,1,0:T(8,128)(2,1)}, bf16[8,2,128,128]{3,2,1,0:T(8,128)(2,1)S(1)}, u32[]{:S(2)}, u32[]{:S(2)}) %collective-permute-start.4) | collective-permute-done | bytes 524320 | tf_op jit(solution)/shard_map/ppermute | solution.py:246
  369.9 4.5 %collective-permute-start.5 = (bf16[8,2,128,128]{3,2,1,0:T(8,128)(2,1)S(1)}, bf16[8,2,128,128]{3,2,1,0:T(8,128)(2,1)S(1)}, u32[]{:S(2)}, u32[]{:S(2)}) collective-permute-start(bf16[8,2,128,128]{3,2,1,0:T(8,128)(2,1)S(1)} %add_convert_fusion.2), channel_id=1, source_target_pairs={{0,127},{8,0},{16,8},{24,16},{32,24},{40,32},{48,40},{56,48},{64,5... | collective-permute-start | bytes 1572872 | tf_op jit(solution)/shard_map/ppermute | solution.py:246
  374.3 5.6 %collective-permute-done.6 = bf16[8,2,128,128]{3,2,1,0:T(8,128)(2,1)S(1)} collective-permute-done((bf16[8,2,128,128]{3,2,1,0:T(8,128)(2,1)}, bf16[8,2,128,128]{3,2,1,0:T(8,128)(2,1)S(1)}, u32[]{:S(2)}, u32[]{:S(2)}) %collective-permute-start.6) | collective-permute-done | bytes 524320 | tf_op jit(solution)/shard_map/ppermute | solution.py:246
  381.1 7.6 %collective-permute-start.7 = (bf16[8,2,128,128]{3,2,1,0:T(8,128)(2,1)S(1)}, bf16[8,2,128,128]{3,2,1,0:T(8,128)(2,1)S(1)}, u32[]{:S(2)}, u32[]{:S(2)}) collective-permute-start(bf16[8,2,128,128]{3,2,1,0:T(8,128)(2,1)S(1)} %add_convert_fusion.1), channel_id=1, source_target_pairs={{0,119},{8,127},{16,0},{24,8},{32,16},{40,24},{48,32},{56,40},{64,... | collective-permute-start | bytes 1572872 | tf_op jit(solution)/shard_map/ppermute | solution.py:246
  388.7 10.1 %collective-permute-done.7 = bf16[8,2,128,128]{3,2,1,0:T(8,128)(2,1)S(1)} collective-permute-done((bf16[8,2,128,128]{3,2,1,0:T(8,128)(2,1)S(1)}, bf16[8,2,128,128]{3,2,1,0:T(8,128)(2,1)S(1)}, u32[]{:S(2)}, u32[]{:S(2)}) %collective-permute-start.7) | collective-permute-done | bytes 524320 | tf_op jit(solution)/shard_map/ppermute | solution.py:246
  401.3 2.6 copy.41
  406.1 2.4 broadcast_select_fusion
  (51 shorter events, 14.5 us)
Async XLA Ops:
  5.2 12.0 %copy-start.9 = (bf16[128,1024]{1,0:T(8,128)(2,1)S(1)}, bf16[128,1024]{1,0:T(8,128)(2,1)}, u32[]{:S(2)}) copy-start(bf16[128,1024]{1,0:T(8,128)(2,1)} %param.6) | copy-start | bytes 786436
  5.2 12.3 %copy-start.10 = (bf16[128,1024]{1,0:T(8,128)(2,1)S(1)}, bf16[128,1024]{1,0:T(8,128)(2,1)}, u32[]{:S(2)}) copy-start(bf16[128,1024]{1,0:T(8,128)(2,1)} %param.7) | copy-start | bytes 786436
  5.2 64.7 %all-to-all-start = ((bf16[128,2,8,1024]{3,2,1,0:T(8,128)(2,1)}), bf16[128,2,8,1024]{3,2,1,0:T(8,128)(2,1)}, u32[]{:S(2)}, u32[]{:S(2)}) async-start(bf16[128,2,8,1024]{3,2,1,0:T(8,128)(2,1)} %pad_maximum_fusion), calls=%async_computation | async-start | bytes 8388608 | tf_op jit(solution)/shard_map/all_to_all | solution.py:250
  69.9 13.9 %all-to-all-start.2 = ((bf16[8,2,128,128]{3,2,1,0:T(8,128)(2,1)}), bf16[8,2,128,128]{3,2,1,0:T(8,128)(2,1)S(1)}, u32[]{:S(2)}, u32[]{:S(2)}) async-start(bf16[8,2,128,128]{3,2,1,0:T(8,128)(2,1)} %pad_maximum_fusion.1.kv0), calls=%async_computation.2 | async-start | bytes 1048576 | tf_op jit(solution)/shard_map/all_to_all | solution.py:250
  83.8 1.6 copy-start.1
  85.4 31.9 %all-to-all-start.1 = ((bf16[16,2,32,1024]{3,2,1,0:T(8,128)(2,1)}), bf16[16,2,32,1024]{3,2,1,0:T(8,128)(2,1)S(1)}, u32[]{:S(2)}, u32[]{:S(2)}) async-start(bf16[16,2,32,1024]{3,2,1,0:T(8,128)(2,1)} %broadcast_in_dim.5), calls=%async_computation.1 | async-start | bytes 4194304 | tf_op jit(solution)/shard_map/all_to_all | solution.py:250
  117.2 1.3 copy-start
  194.1 23.1 %all-to-all-start.5 = ((bf16[8,2,128,128]{3,2,1,0:T(8,128)(2,1)}), bf16[8,2,128,128]{3,2,1,0:T(8,128)(2,1)S(1)}, u32[]{:S(2)}, u32[]{:S(2)}) async-start(bf16[8,2,128,128]{3,2,1,0:T(8,128)(2,1)} %get-tuple-element.21), calls=%async_computation.5 | async-start | bytes 1048576 | tf_op jit(solution)/shard_map/all_to_all | solution.py:250
  217.2 184.1 %all-to-all-start.4 = ((bf16[128,2,8,1024]{3,2,1,0:T(8,128)(2,1)}), bf16[128,2,8,1024]{3,2,1,0:T(8,128)(2,1)}, u32[]{:S(2)}, u32[]{:S(2)}) async-start(bf16[128,2,8,1024]{3,2,1,0:T(8,128)(2,1)} %concatenate.12.clone), calls=%async_computation.4 | async-start | bytes 8388608 | tf_op jit(solution)/shard_map/all_to_all | solution.py:250
  222.7 55.8 %collective-permute-start = (bf16[8,2,128,128]{3,2,1,0:T(8,128)(2,1)}, bf16[8,2,128,128]{3,2,1,0:T(8,128)(2,1)S(1)}, u32[]{:S(2)}, u32[]{:S(2)}) collective-permute-start(bf16[8,2,128,128]{3,2,1,0:T(8,128)(2,1)} %pad_maximum_fusion.1.kv0), channel_id=1, source_target_pairs={{0,8},{8,16},{16,24},{24,32},{32,40},{40,48},{48,56},{56,64},{64,7... | collective-permute-start | bytes 1572872 | tf_op jit(solution)/shard_map/ppermute | solution.py:246
  224.7 68.0 %collective-permute-start.1 = (bf16[8,2,128,128]{3,2,1,0:T(8,128)(2,1)}, bf16[8,2,128,128]{3,2,1,0:T(8,128)(2,1)S(1)}, u32[]{:S(2)}, u32[]{:S(2)}) collective-permute-start(bf16[8,2,128,128]{3,2,1,0:T(8,128)(2,1)} %pad_maximum_fusion.1.kv0), channel_id=1, source_target_pairs={{0,16},{8,24},{16,32},{24,40},{32,48},{40,56},{48,64},{56,72},{64,... | collective-permute-start | bytes 1572872 | tf_op jit(solution)/shard_map/ppermute | solution.py:246
  278.5 33.7 %copy-start.5 = (bf16[8,2,128,128]{3,2,1,0:T(8,128)(2,1)}, bf16[8,2,128,128]{3,2,1,0:T(8,128)(2,1)S(1)}, u32[]{:S(2)}) copy-start(bf16[8,2,128,128]{3,2,1,0:T(8,128)(2,1)S(1)} %collective-permute-done.kv1) | copy-start | bytes 1572868
  278.5 22.5 %collective-permute-start.2 = (bf16[8,2,128,128]{3,2,1,0:T(8,128)(2,1)S(1)}, bf16[8,2,128,128]{3,2,1,0:T(8,128)(2,1)S(1)}, u32[]{:S(2)}, u32[]{:S(2)}) collective-permute-start(bf16[8,2,128,128]{3,2,1,0:T(8,128)(2,1)S(1)} %collective-permute-done.kv1), channel_id=1, source_target_pairs={{0,16},{8,24},{16,32},{24,40},{32,48},{40,56},{48,64},{56,72},{64,... | collective-permute-start | bytes 1572872 | tf_op jit(solution)/shard_map/ppermute | solution.py:246
  292.7 19.5 %copy-start.6 = (bf16[8,2,128,128]{3,2,1,0:T(8,128)(2,1)}, bf16[8,2,128,128]{3,2,1,0:T(8,128)(2,1)S(1)}, u32[]{:S(2)}) copy-start(bf16[8,2,128,128]{3,2,1,0:T(8,128)(2,1)S(1)} %collective-permute-done.1.kv2) | copy-start | bytes 1572868
  292.7 19.5 %collective-permute-start.3 = (bf16[8,2,128,128]{3,2,1,0:T(8,128)(2,1)S(1)}, bf16[8,2,128,128]{3,2,1,0:T(8,128)(2,1)S(1)}, u32[]{:S(2)}, u32[]{:S(2)}) collective-permute-start(bf16[8,2,128,128]{3,2,1,0:T(8,128)(2,1)S(1)} %collective-permute-done.1.kv2), channel_id=1, source_target_pairs={{0,16},{8,24},{16,32},{24,40},{32,48},{40,56},{48,64},{56,72},{64,... | collective-permute-start | bytes 1572872 | tf_op jit(solution)/shard_map/ppermute | solution.py:246
  301.0 11.2 %copy-start.7 = (bf16[8,2,128,128]{3,2,1,0:T(8,128)(2,1)}, bf16[8,2,128,128]{3,2,1,0:T(8,128)(2,1)S(1)}, u32[]{:S(2)}) copy-start(bf16[8,2,128,128]{3,2,1,0:T(8,128)(2,1)S(1)} %collective-permute-done.2.kv3) | copy-start | bytes 1572868
  312.2 0.8 copy-start.8
  354.4 44.4 %copy-start.4 = (bf16[8,2,128,128]{3,2,1,0:T(8,128)(2,1)S(1)}, bf16[8,2,128,128]{3,2,1,0:T(8,128)(2,1)}, u32[]{:S(2)}) copy-start(bf16[8,2,128,128]{3,2,1,0:T(8,128)(2,1)} %get-tuple-element.16) | copy-start | bytes 1572868
  354.4 14.3 %collective-permute-start.4 = (bf16[8,2,128,128]{3,2,1,0:T(8,128)(2,1)}, bf16[8,2,128,128]{3,2,1,0:T(8,128)(2,1)S(1)}, u32[]{:S(2)}, u32[]{:S(2)}) collective-permute-start(bf16[8,2,128,128]{3,2,1,0:T(8,128)(2,1)} %get-tuple-element.18), channel_id=1, source_target_pairs={{0,119},{8,127},{16,0},{24,8},{32,16},{40,24},{48,32},{56,40},{64,... | collective-permute-start | bytes 1572872 | tf_op jit(solution)/shard_map/ppermute | solution.py:246
  357.4 22.5 %collective-permute-start.6 = (bf16[8,2,128,128]{3,2,1,0:T(8,128)(2,1)}, bf16[8,2,128,128]{3,2,1,0:T(8,128)(2,1)S(1)}, u32[]{:S(2)}, u32[]{:S(2)}) collective-permute-start(bf16[8,2,128,128]{3,2,1,0:T(8,128)(2,1)} %get-tuple-element.20), channel_id=1, source_target_pairs={{0,119},{8,127},{16,0},{24,8},{32,16},{40,24},{48,32},{56,40},{64,... | collective-permute-start | bytes 1572872 | tf_op jit(solution)/shard_map/ppermute | solution.py:246
  369.9 18.8 %collective-permute-start.5 = (bf16[8,2,128,128]{3,2,1,0:T(8,128)(2,1)S(1)}, bf16[8,2,128,128]{3,2,1,0:T(8,128)(2,1)S(1)}, u32[]{:S(2)}, u32[]{:S(2)}) collective-permute-start(bf16[8,2,128,128]{3,2,1,0:T(8,128)(2,1)S(1)} %add_convert_fusion.2), channel_id=1, source_target_pairs={{0,127},{8,0},{16,8},{24,16},{32,24},{40,32},{48,40},{56,48},{64,5... | collective-permute-start | bytes 1572872 | tf_op jit(solution)/shard_map/ppermute | solution.py:246
  381.1 17.7 %collective-permute-start.7 = (bf16[8,2,128,128]{3,2,1,0:T(8,128)(2,1)S(1)}, bf16[8,2,128,128]{3,2,1,0:T(8,128)(2,1)S(1)}, u32[]{:S(2)}, u32[]{:S(2)}) collective-permute-start(bf16[8,2,128,128]{3,2,1,0:T(8,128)(2,1)S(1)} %add_convert_fusion.1), channel_id=1, source_target_pairs={{0,119},{8,127},{16,0},{24,8},{32,16},{40,24},{48,32},{56,40},{64,... | collective-permute-start | bytes 1572872 | tf_op jit(solution)/shard_map/ppermute | solution.py:246
  403.9 1.6 copy-start.2
  403.9 2.2 copy-start.3
